TPU v7x, 1024 devices: a whole 4x8x16 slice. The times are simulated.
1024 devices in a mesh: ex: 64 (over z, y_hi), ez: 16 (over y_lo, x, core).
Axes of the slice: x: 4, y: 8 (y_hi: 4, y_lo: 2; y = y_hi * 2 + y_lo), z: 16, core: 2. Of those that a mesh axis runs over, the one named last changes fastest.
Arguments:
- potential: float32 [512, 16, 128], P('ex', None, 'ez'), may hold values from -1.5 to 0.5
- basis_start: bfloat16 [64, 16, 2, 1728, 128], P('ex', 'ez'), may hold values from -6 to 6
Outputs:
- diagonal_blocks: float32 [64, 128, 16, 2, 128], P('ex', 'ez')
- coupling_blocks: float32 [64, 128, 16, 2, 3, 128], P('ex', 'ez')
All inputs are finite; a program needn't handle non-finite values.
Results may differ from a plain program's by a relative error of at most 0.0003.
Values sent between devices are 32-bit elements; how exact they have to be, the bound alone decides.
A program may use at most 32 MiB of HBM per device.

v0:
```python
import jax
import jax.numpy as jnp
from jax import lax
from jax.sharding import PartitionSpec as P

G = 8
FILTER = 3


center = 6.5
halfwidth = 5.5
penalty = 1.0
highest = lax.Precision.HIGHEST


def padded_2(cells, sides, width):
    for axis, dim in sides:
        count = lax.axis_size(axis)
        head = lax.slice_in_dim(cells, 0, width, axis=dim)
        tail = lax.slice_in_dim(cells, cells.shape[dim] - width, cells.shape[dim], axis=dim)
        cells = jnp.concatenate(
            [
                lax.ppermute(tail, axis, [(i, (i + 1) % count) for i in range(count)]),
                cells,
                lax.ppermute(head, axis, [((i + 1) % count, i) for i in range(count)]),
            ],
            axis=dim,
        )
    return cells


def from_behind(block, axis, distance):
    devices = range(lax.axis_size(axis))
    route = [((i - distance) % len(devices), i) for i in devices]
    return lax.ppermute(block, axis, route)


def apply_hamiltonian(field, potential_box):
    padded = jnp.pad(field, ((1, 1), (1, 1), (1, 1), (0, 0)))
    beside = padded[2:, 1:-1, 1:-1] + padded[:-2, 1:-1, 1:-1]
    beside = beside + padded[1:-1, 2:, 1:-1] + padded[1:-1, :-2, 1:-1]
    beside = beside + padded[1:-1, 1:-1, 2:] + padded[1:-1, 1:-1, :-2]
    return 3.0 * field - 0.5 * beside + potential_box[:, :, :, None] * field


def local_basis(initial, potential_box):
    box_side = potential_box.shape[0]
    margin = (box_side - G) // 2
    columns = initial.shape[-1]
    previous = initial.astype(jnp.float32).reshape(box_side, box_side, box_side, columns)
    current = (apply_hamiltonian(previous, potential_box) - center * previous) / halfwidth
    for iteration in range(FILTER - 1):
        following = (
            2.0 / halfwidth * (apply_hamiltonian(current, potential_box) - center * current)
            - previous
        )
        previous, current = (current, following)
    flattened = current.reshape(box_side**3, columns)
    intersection = lax.dot_general(
        flattened,
        flattened,
        (((0,), (0,)), ((), ())),
        precision=highest,
        preferred_element_type=jnp.float32,
    )
    factor = jnp.linalg.cholesky(intersection)
    interior = current[margin : margin + G, margin : margin + G, margin : margin + G].reshape(
        G**3, columns
    )
    solved = jax.scipy.linalg.solve_triangular(factor, interior.T, lower=True)
    return solved.T.reshape(G, G, G, columns)


def forward_difference(basis, dimension):
    differences = jnp.diff(basis, axis=dimension)
    widths = [(0, 0)] * basis.ndim
    widths[dimension] = (0, 1)
    return jnp.pad(differences, widths)


def volume_terms(basis, inner_potential):
    gradients = [forward_difference(basis, dimension) for dimension in (1, 2, 3)]
    weighted = jnp.concatenate(
        [
            0.5 * gradients[0],
            0.5 * gradients[1],
            0.5 * gradients[2],
            inner_potential[..., None] * basis,
        ],
        axis=1,
    )
    plain_side = jnp.concatenate(gradients + [basis], axis=1)
    elements = basis.shape[0]
    columns = basis.shape[-1]
    weighted = weighted.reshape(elements, -1, columns)
    plain_side = plain_side.reshape(elements, -1, columns)
    return jnp.einsum("epi,epj->iej", weighted, plain_side, precision=highest)


def face_traces(basis):
    points = basis.shape[1]
    elements = basis.shape[0]
    columns = basis.shape[-1]
    plus_layers = []
    minus_layers = []
    for dimension in (1, 2, 3):
        outer_last = lax.index_in_dim(basis, points - 1, dimension, keepdims=False)
        inner_last = lax.index_in_dim(basis, points - 2, dimension, keepdims=False)
        outer_first = lax.index_in_dim(basis, 0, dimension, keepdims=False)
        inner_first = lax.index_in_dim(basis, 1, dimension, keepdims=False)
        plus_layers.append(jnp.stack([outer_last, outer_last - inner_last], axis=1))
        minus_layers.append(jnp.stack([outer_first, inner_first - outer_first], axis=1))
    plus_traces = jnp.stack(plus_layers, axis=1).reshape(elements, 3, 2, points * points, columns)
    minus_traces = jnp.stack(minus_layers, axis=1).reshape(elements, 3, 2, points * points, columns)
    return (plus_traces, minus_traces)


def face_diagonal(plus_traces, minus_traces):
    side_plus = -0.25 * plus_traces[:, :, 1] + 0.5 * penalty * plus_traces[:, :, 0]
    side_minus = 0.25 * minus_traces[:, :, 1] + 0.5 * penalty * minus_traces[:, :, 0]
    direct = jnp.einsum("ekpi,ekpj->iej", side_plus, plus_traces[:, :, 0], precision=highest)
    direct = direct + jnp.einsum(
        "ekpi,ekpj->iej", side_minus, minus_traces[:, :, 0], precision=highest
    )
    mirror = jnp.einsum("ekpi,ekpj->iej", plus_traces[:, :, 0], side_plus, precision=highest)
    mirror = mirror + jnp.einsum(
        "ekpi,ekpj->iej", minus_traces[:, :, 0], side_minus, precision=highest
    )
    return direct + mirror


def coupling(plus_traces, next_traces):
    weighted = 0.25 * plus_traces[:, :, 1] - penalty * plus_traces[:, :, 0]
    result = jnp.einsum("ekpi,ekpj->iekj", weighted, next_traces[:, :, 0], precision=highest)
    return result - 0.25 * jnp.einsum(
        "ekpi,ekpj->iekj", plus_traces[:, :, 0], next_traces[:, :, 1], precision=highest
    )


def local(potential, basis_start):
    y_elements = basis_start.shape[2]
    columns = basis_start.shape[-1]
    margin = G // 4
    box_side = G + 2 * margin
    extended = padded_2(potential, (("ex", 0), ("ez", 2)), margin)
    extended = jnp.concatenate([extended[:, -margin:], extended, extended[:, :margin]], axis=1)
    starts = basis_start.reshape(y_elements, box_side**3, columns)

    def one_element(element):
        initial = lax.dynamic_index_in_dim(starts, element, 0, keepdims=False)
        potential_box = lax.dynamic_slice_in_dim(extended, element * G, box_side, 1)
        return local_basis(initial, potential_box)

    basis = lax.map(one_element, jnp.arange(y_elements, dtype=jnp.int32))
    inner_potential = potential.reshape(G, y_elements, G, G).transpose(1, 0, 2, 3)
    plus_traces, minus_traces = face_traces(basis)
    diagonal = volume_terms(basis, inner_potential) + face_diagonal(plus_traces, minus_traces)
    diagonal = diagonal[None, :, None]
    from_x = from_behind(minus_traces[:, 0], "ex", -1)
    from_z = from_behind(minus_traces[:, 2], "ez", -1)
    from_y = jnp.roll(minus_traces[:, 1], -1, axis=0)
    next_traces = jnp.stack([from_x, from_y, from_z], axis=1)
    coupled = coupling(plus_traces, next_traces)[None, :, None]
    diagonal_rows, coupling_rows = (
        lax.all_to_all(diagonal, "ez", split_axis=1, concat_axis=2, tiled=True),
        lax.all_to_all(coupled, "ez", split_axis=1, concat_axis=2, tiled=True),
    )
    return (diagonal_rows, coupling_rows)


def solution(mesh):
    return jax.shard_map(
        local,
        mesh=mesh,
        in_specs=(P("ex", None, "ez"), P("ex", "ez", None, None, None)),
        out_specs=(P("ex", "ez", None, None, None), P("ex", "ez", None, None, None, None)),
        check_vma=False,
    )
```

profile of v0, /device:TPU:1, one launch (start us, length us, event | category | flops | bytes accessed | tf_op | source)
XLA Modules:
  0.0 150.8 jit_solution(539401688873399035)
XLA Ops:
  0.6 0.8 copy.51
  1.5 5.0 %collective-permute-start = (f32[2,16,8]{2,1,0:T(8,128)S(1)}, f32[2,16,8]{2,1,0:T(8,128)S(1)}, u32[]{:S(2)}, u32[]{:S(2)}) collective-permute-start(f32[2,16,8]{2,1,0:T(8,128)S(1)} %get-tuple-element.114), channel_id=1, source_target_pairs={{0,16},{16,32},{32,48},{48,64},{64,80},{80,96},{96,112},{112,128},... | collective-permute-start | bytes 3080 | tf_op jit(solution)/shard_map/ppermute | solution.py:23
  6.5 19.3 %collective-permute-start.1 = (f32[2,16,8]{2,1,0:T(8,128)S(1)}, f32[2,16,8]{2,1,0:T(8,128)S(1)}, u32[]{:S(2)}, u32[]{:S(2)}) collective-permute-start(f32[2,16,8]{2,1,0:T(8,128)S(1)} %get-tuple-element.115), channel_id=1, source_target_pairs={{16,0},{32,16},{48,32},{64,48},{80,64},{96,80},{112,96},{128,112},... | collective-permute-start | bytes 3080 | tf_op jit(solution)/shard_map/ppermute | solution.py:25
  25.9 0.8 collective-permute-done.1
  26.8 4.5 %collective-permute-start.2 = (f32[12,16,2]{2,1,0:T(8,128)S(1)}, f32[12,16,2]{2,1,0:T(8,128)S(1)}, u32[]{:S(2)}, u32[]{:S(2)}) collective-permute-start(f32[12,16,2]{2,1,0:T(8,128)S(1)} %get-tuple-element.112), channel_id=1, source_target_pairs={{0,1},{1,2},{2,3},{3,4},{4,5},{5,6},{6,7},{7,8},{8,9},{9,10},{10,1... | collective-permute-start | bytes 4616 | tf_op jit(solution)/shard_map/ppermute | solution.py:23
  31.4 1.9 %collective-permute-start.3 = (f32[12,16,2]{2,1,0:T(8,128)S(1)}, f32[12,16,2]{2,1,0:T(8,128)S(1)}, u32[]{:S(2)}, u32[]{:S(2)}) collective-permute-start(f32[12,16,2]{2,1,0:T(8,128)S(1)} %get-tuple-element.113), channel_id=1, source_target_pairs={{1,0},{2,1},{3,2},{4,3},{5,4},{6,5},{7,6},{8,7},{9,8},{10,9},{11,1... | collective-permute-start | bytes 4616 | tf_op jit(solution)/shard_map/ppermute | solution.py:25
  33.3 0.9 reshape.199
  34.3 3.0 %collective-permute-done.3 = f32[12,16,2]{2,1,0:T(8,128)S(1)} collective-permute-done((f32[12,16,2]{2,1,0:T(8,128)S(1)}, f32[12,16,2]{2,1,0:T(8,128)S(1)}, u32[]{:S(2)}, u32[]{:S(2)}) %collective-permute-start.3) | collective-permute-done | bytes 1568 | tf_op jit(solution)/shard_map/ppermute | solution.py:25
  37.5 66.3 %while.12 = (s32[]{:T(128)}, f32[2,8,8,8,128]{4,3,2,1,0:T(8,128)S(1)}, s32[2]{0:T(128)S(1)}, bf16[2,1728,128]{2,1,0:T(8,128)(2,1)}, f32[12,20,12]{2,1,0:T(8,128)...) while((s32[]{:T(128)}, f32[2,8,8,8,128]{4,3,2,1,0:T(8,128)S(1)}, s32[2]{0:T(128)S(1)}, ...), condition=%wide.region_3.4_spmd, body=%wide.region_0.3_spmd.sunk | while | flops 450062144 | bytes 14051031 | solution.py:154
  37.5 0.6 dynamic_slice.26
  40.7 1.1 dynamic-slice_convert_fusion.2
  41.9 1.0 broadcast_multiply_fusion.9
  43.0 1.2 fusion.95
  44.1 1.2 fusion.96
  45.3 2.0 %convolution_bitcast_fusion.7 = f32[128,128]{1,0:T(8,128)S(1)} fusion(f32[12,12,12,128]{3,2,1,0:T(8,128)S(1)} %fusion.96), kind=kOutput, calls=%fused_computation.51.clone.1 | convolution fusion | flops 339738624 | bytes 950272 | tf_op jit(solution)/shard_map/while/body/eval_jaxpr/dot_general | solution.py:59
  47.4 11.7 %cholesky.58 = f32[128,128]{1,0:T(8,128)S(1)} custom-call(f32[128,128]{1,0:T(8,128)S(1)} %fusion.97), custom_call_target="Cholesky" | custom-call | tf_op jit(solution)/shard_map/while/body/eval_jaxpr/jit(cholesky)/cholesky | solution.py:66
  59.2 0.6 compare_reduce_fusion.2
  59.8 0.7 fusion.98
  60.5 9.8 %custom-call.15 = f32[1,128,128]{1,2,0:T(8,128)S(1)} custom-call(f32[1,128,128]{2,1,0:T(8,128)S(1)} %fusion.98), custom_call_target="InvertDiagBlocksLowerTriangular" | custom-call | tf_op jit(solution)/shard_map/while/body/eval_jaxpr/jit(_solve_triangular)/triangular_solve | solution.py:70
  70.3 0.4 fusion.99
  70.7 0.6 dynamic_slice.26
  73.9 1.1 dynamic-slice_convert_fusion.2
  75.1 1.0 broadcast_multiply_fusion.9
  76.1 1.2 fusion.95
  77.3 1.2 fusion.96
  78.5 2.0 %convolution_bitcast_fusion.7 = f32[128,128]{1,0:T(8,128)S(1)} fusion(f32[12,12,12,128]{3,2,1,0:T(8,128)S(1)} %fusion.96), kind=kOutput, calls=%fused_computation.51.clone.1 | convolution fusion | flops 339738624 | bytes 950272 | tf_op jit(solution)/shard_map/while/body/eval_jaxpr/dot_general | solution.py:59
  80.6 11.7 %cholesky.58 = f32[128,128]{1,0:T(8,128)S(1)} custom-call(f32[128,128]{1,0:T(8,128)S(1)} %fusion.97), custom_call_target="Cholesky" | custom-call | tf_op jit(solution)/shard_map/while/body/eval_jaxpr/jit(cholesky)/cholesky | solution.py:66
  92.4 0.6 compare_reduce_fusion.2
  93.0 0.7 fusion.98
  93.7 9.8 %custom-call.15 = f32[1,128,128]{1,2,0:T(8,128)S(1)} custom-call(f32[1,128,128]{2,1,0:T(8,128)S(1)} %fusion.98), custom_call_target="InvertDiagBlocksLowerTriangular" | custom-call | tf_op jit(solution)/shard_map/while/body/eval_jaxpr/jit(_solve_triangular)/triangular_solve | solution.py:70
  103.5 0.4 fusion.99
  104.3 0.7 convolution_bitcast_fusion.4
  105.0 0.7 convolution_bitcast_fusion.2
  105.9 2.8 %collective-permute-start.5 = (f32[2,2,64,128]{3,2,0,1:T(8,128)S(1)}, f32[2,2,64,128]{3,2,0,1:T(8,128)S(1)}, u32[]{:S(2)}, u32[]{:S(2)}) collective-permute-start(f32[2,2,64,128]{3,2,0,1:T(8,128)S(1)} %pad_maximum_fusion.13), channel_id=1, source_target_pairs={{1,0},{2,1},{3,2},{4,3},{5,4},{6,5},{7,6},{8,7},{9,8},{10,9},{11,1... | collective-permute-start | bytes 393224 | tf_op jit(solution)/shard_map/ppermute | solution.py:35
  108.7 8.4 %collective-permute-start.4 = (f32[2,2,64,128]{3,2,0,1:T(8,128)S(1)}, f32[2,2,64,128]{3,2,0,1:T(8,128)S(1)}, u32[]{:S(2)}, u32[]{:S(2)}) collective-permute-start(f32[2,2,64,128]{3,2,0,1:T(8,128)S(1)} %get-tuple-element.108), channel_id=1, source_target_pairs={{16,0},{32,16},{48,32},{64,48},{80,64},{96,80},{112,96},{128,112},... | collective-permute-start | bytes 393224 | tf_op jit(solution)/shard_map/ppermute | solution.py:35
  117.1 0.7 fusion.40
  117.8 0.7 fusion.39
  119.4 3.5 %fusion.37 = f32[1,128,1,2,128]{1,4,3,2,0:T(8,128)S(1)} fusion(f32[2,128,128]{2,1,0:T(8,128)S(1)} %fusion.39, f32[2,2048,128]{2,1,0:T(8,128)S(1)} %bitcast.163, f32[2,2048,128]{2,1,0:T(8,128)S(1)} %bitcast.164), kind=kOutput, calls=%fused_computation.76 | convolution fusion | flops 805339136 | bytes 4456448 | tf_op jit(solution)/shard_map/epi,epj->iej/dot_general | solution.py:97
  122.9 0.8 copy.59
  123.7 7.5 %all-to-all-start = ((f32[1,128,1,2,128]{4,3,2,0,1:T(2,128)}), f32[1,128,1,2,128]{4,3,2,0,1:T(2,128)S(1)}, u32[]{:S(2)}, u32[]{:S(2)}) async-start(f32[1,128,1,2,128]{4,3,2,0,1:T(2,128)} %copy.59), calls=%async_computation | async-start | bytes 262144 | tf_op jit(solution)/shard_map/all_to_all | solution.py:165
  131.3 0.8 convolution_multiply_fusion
  132.1 0.8 fusion.36
  132.9 0.9 copy.62
  133.8 3.6 %all-to-all-done = f32[1,128,1,2,128]{4,3,2,0,1:T(2,128)S(1)} async-done(((f32[1,128,1,2,128]{4,3,2,0,1:T(2,128)}), f32[1,128,1,2,128]{4,3,2,0,1:T(2,128)S(1)}, u32[]{:S(2)}, u32[]{:S(2)}) %all-to-all-start) | async-done | bytes 131104 | tf_op jit(solution)/shard_map/all_to_all | solution.py:165
  137.4 4.0 %all-to-all-start.1 = ((f32[1,128,1,2,3,128]{5,3,4,2,0,1:T(2,128)}), f32[1,128,1,2,3,128]{5,3,4,2,0,1:T(2,128)S(1)}, u32[]{:S(2)}, u32[]{:S(2)}) async-start(f32[1,128,1,2,3,128]{5,3,4,2,0,1:T(2,128)} %copy.62), calls=%async_computation.1 | async-start | bytes 786432 | tf_op jit(solution)/shard_map/all_to_all | solution.py:166
  141.4 0.8 copy.64
  142.2 7.6 %all-to-all-done.1 = f32[1,128,1,2,3,128]{5,3,4,2,0,1:T(2,128)S(1)} async-done(((f32[1,128,1,2,3,128]{5,3,4,2,0,1:T(2,128)}), f32[1,128,1,2,3,128]{5,3,4,2,0,1:T(2,128)S(1)}, u32[]{:S(2)}, u32[]{:S(2)}) %all-to-all-start.1) | async-done | bytes 393248 | tf_op jit(solution)/shard_map/all_to_all | solution.py:166
  149.8 1.1 copy.65
  (46 shorter events, 2.4 us)
Async XLA Ops:
  1.5 24.4 %collective-permute-start = (f32[2,16,8]{2,1,0:T(8,128)S(1)}, f32[2,16,8]{2,1,0:T(8,128)S(1)}, u32[]{:S(2)}, u32[]{:S(2)}) collective-permute-start(f32[2,16,8]{2,1,0:T(8,128)S(1)} %get-tuple-element.114), channel_id=1, source_target_pairs={{0,16},{16,32},{32,48},{48,64},{64,80},{80,96},{96,112},{112,128},... | collective-permute-start | bytes 3080 | tf_op jit(solution)/shard_map/ppermute | solution.py:23
  6.5 20.2 %collective-permute-start.1 = (f32[2,16,8]{2,1,0:T(8,128)S(1)}, f32[2,16,8]{2,1,0:T(8,128)S(1)}, u32[]{:S(2)}, u32[]{:S(2)}) collective-permute-start(f32[2,16,8]{2,1,0:T(8,128)S(1)} %get-tuple-element.115), channel_id=1, source_target_pairs={{16,0},{32,16},{48,32},{64,48},{80,64},{96,80},{112,96},{128,112},... | collective-permute-start | bytes 3080 | tf_op jit(solution)/shard_map/ppermute | solution.py:25
  26.8 7.4 %collective-permute-start.2 = (f32[12,16,2]{2,1,0:T(8,128)S(1)}, f32[12,16,2]{2,1,0:T(8,128)S(1)}, u32[]{:S(2)}, u32[]{:S(2)}) collective-permute-start(f32[12,16,2]{2,1,0:T(8,128)S(1)} %get-tuple-element.112), channel_id=1, source_target_pairs={{0,1},{1,2},{2,3},{3,4},{4,5},{5,6},{6,7},{7,8},{8,9},{9,10},{10,1... | collective-permute-start | bytes 4616 | tf_op jit(solution)/shard_map/ppermute | solution.py:23
  31.4 5.9 %collective-permute-start.3 = (f32[12,16,2]{2,1,0:T(8,128)S(1)}, f32[12,16,2]{2,1,0:T(8,128)S(1)}, u32[]{:S(2)}, u32[]{:S(2)}) collective-permute-start(f32[12,16,2]{2,1,0:T(8,128)S(1)} %get-tuple-element.113), channel_id=1, source_target_pairs={{1,0},{2,1},{3,2},{4,3},{5,4},{6,5},{7,6},{8,7},{9,8},{10,9},{11,1... | collective-permute-start | bytes 4616 | tf_op jit(solution)/shard_map/ppermute | solution.py:25
  105.9 25.4 %collective-permute-start.5 = (f32[2,2,64,128]{3,2,0,1:T(8,128)S(1)}, f32[2,2,64,128]{3,2,0,1:T(8,128)S(1)}, u32[]{:S(2)}, u32[]{:S(2)}) collective-permute-start(f32[2,2,64,128]{3,2,0,1:T(8,128)S(1)} %pad_maximum_fusion.13), channel_id=1, source_target_pairs={{1,0},{2,1},{3,2},{4,3},{5,4},{6,5},{7,6},{8,7},{9,8},{10,9},{11,1... | collective-permute-start | bytes 393224 | tf_op jit(solution)/shard_map/ppermute | solution.py:35
  108.7 22.5 %collective-permute-start.4 = (f32[2,2,64,128]{3,2,0,1:T(8,128)S(1)}, f32[2,2,64,128]{3,2,0,1:T(8,128)S(1)}, u32[]{:S(2)}, u32[]{:S(2)}) collective-permute-start(f32[2,2,64,128]{3,2,0,1:T(8,128)S(1)} %get-tuple-element.108), channel_id=1, source_target_pairs={{16,0},{32,16},{48,32},{64,48},{80,64},{96,80},{112,96},{128,112},... | collective-permute-start | bytes 393224 | tf_op jit(solution)/shard_map/ppermute | solution.py:35
  123.7 13.7 %all-to-all-start = ((f32[1,128,1,2,128]{4,3,2,0,1:T(2,128)}), f32[1,128,1,2,128]{4,3,2,0,1:T(2,128)S(1)}, u32[]{:S(2)}, u32[]{:S(2)}) async-start(f32[1,128,1,2,128]{4,3,2,0,1:T(2,128)} %copy.59), calls=%async_computation | async-start | bytes 262144 | tf_op jit(solution)/shard_map/all_to_all | solution.py:165
  137.4 12.4 %all-to-all-start.1 = ((f32[1,128,1,2,3,128]{5,3,4,2,0,1:T(2,128)}), f32[1,128,1,2,3,128]{5,3,4,2,0,1:T(2,128)S(1)}, u32[]{:S(2)}, u32[]{:S(2)}) async-start(f32[1,128,1,2,3,128]{5,3,4,2,0,1:T(2,128)} %copy.62), calls=%async_computation.1 | async-start | bytes 786432 | tf_op jit(solution)/shard_map/all_to_all | solution.py:166
where the time goes:
time: 152 us; the launch traced here: 151 us
  other arithmetic  56.1 us (37%)
  starting transfers between devices  53.6 us (35%)
  waiting for transfers between devices  15 us (10%)
  matrix products  12.6 us (8%)
  local copies, waits for them, and re-layouts  7.09 us (5%)
  loops' own time  5.39 us (4%)
    another operation x6, other arithmetic, local_basis(): factor = jnp.linalg.cholesky(intersection)  24.8 us
    ppermute x2, starting transfers between devices, padded_2(): lax.ppermute(head, axis, [((i + 1) % count, i) for i in range(count)])  21.3 us
    another operation x4, other arithmetic, local_basis(): solved = jax.scipy.linalg.solve_triangular(factor, interior.T, lower=True)  20.9 us
    ppermute x2, starting transfers between devices, from_behind(): return lax.ppermute(block, axis, route)  11.2 us
    ppermute x2, starting transfers between devices, padded_2(): lax.ppermute(tail, axis, [(i, (i + 1) % count) for i in range(count)])  9.57 us
    all_to_all x1, waiting for transfers between devices, local(): lax.all_to_all(coupled, 'ez', split_axis=1, concat_axis=2, tiled=True)  7.58 us
    all_to_all x1, starting transfers between devices, local(): lax.all_to_all(diagonal, 'ez', split_axis=1, concat_axis=2, tiled=True)  7.53 us
    another operation x1, loops' own time, local(): basis = lax.map(one_element, jnp.arange(y_elements, dtype=jnp.int32))  5.39 us
  transfers between devices with their start and end apart: 8, of which 4 were waited for; matrix products, arithmetic and copies ran while one was open for 7% of the time, Pallas kernels for 0%

commit v1 on v0

v1 whole, which is shorter than its diff:
```python
import jax
import jax.numpy as jnp
from jax import lax
from jax.experimental import pallas as pl
from jax.experimental.pallas import tpu as pltpu
from jax.sharding import PartitionSpec as P

G, BOX, NB, EY = 8, 12, 128, 2
ROWS = BOX ** 3
SLAB = BOX * BOX
BLOCKS = NB // 8
HIGHEST = lax.Precision.HIGHEST
F32 = jnp.float32
BF16 = jnp.bfloat16
MESH = pl.DeviceIdType.MESH


def dot(a, b, dims):
    return lax.dot_general(a, b, (dims, ((), ())), precision=HIGHEST, preferred_element_type=F32)


def sub_row(tile, row):
    return jnp.broadcast_to(tile[row:row + 1, :], (8, NB))


def lane_col(tile, lane):
    return jnp.broadcast_to(tile[:, lane:lane + 1], (8, NB))


def factor_inverse(tiles_of, inv_ref):
    sub = lax.broadcasted_iota(jnp.int32, (8, NB), 0)
    lane = lax.broadcasted_iota(jnp.int32, (8, NB), 1)
    tiles = [list(t) for t in tiles_of]
    for k in range(BLOCKS):
        inside = (lane >= 8 * k) & (lane < 8 * k + 8)
        for e in range(len(tiles)):
            T = tiles[e]
            C = [lane_col(T[k], 8 * k + m) for m in range(8)]
            J = jnp.where(inside, jnp.where(lane - 8 * k == sub, 1.0, 0.0).astype(F32), T[k])
            forward = J
            rdiag = jnp.zeros((8, NB), F32)
            for j in range(8):
                r = 1.0 / sub_row(C[j], j)
                mult = jnp.where(sub == j, 0.0, C[j] * r)
                row = sub_row(J, j)
                forward = jnp.where(sub == j, J, forward)
                rdiag = jnp.where(sub == j, r, rdiag)
                for m in range(j + 1, 8):
                    C[m] = C[m] - mult * sub_row(C[m], j)
                J = J - mult * row
            J = J * rdiag
            inv_ref[e, 8 * k:8 * k + 8, :] = jnp.where(lane <= sub + 8 * k, forward * jnp.sqrt(rdiag), 0.0)
            if k + 1 < BLOCKS:
                rows = [sub_row(J, m) for m in range(8)]
                for t in range(k + 1, BLOCKS):
                    old = T[t]
                    new = jnp.where(inside, 0.0, old)
                    for m in range(8):
                        new = new - lane_col(old, 8 * k + m) * rows[m]
                    T[t] = new


def local_kernel(pot_ref, basis_ref, first_ref, left_ref, right_ref,
                 scaled, fa, fb, inner, stencil, gram, inv, traces):
    sub = lax.broadcasted_iota(jnp.int32, (8, NB), 0)
    zero_slab = jnp.zeros((SLAB, NB), F32)
    for buf in (fa, fb):
        for e in range(EY):
            buf[e, 0:SLAB, :] = zero_slab
            buf[e, SLAB + ROWS:2 * SLAB + ROWS, :] = zero_slab

    @pl.loop(0, BOX)
    def _(x):
        low = (pot_ref[x, 0:8, :] - 3.5) * (1.0 / 5.5)
        high = (pot_ref[x, 8:16, :] - 3.5) * (1.0 / 5.5)
        for y in range(16):
            a = lane_col(low, y)
            b = lane_col(high, y)
            for e in range(EY):
                at = (y - 8 * e + 2) % 16
                if at < BOX:
                    base = x * SLAB + at * BOX
                    scaled[e, pl.ds(base, 8), :] = a
                    scaled[e, pl.ds(base + 8, 4), :] = b[0:4, :]

    @pl.loop(0, BOX)
    def _(x):
        for e in range(EY):
            base = pl.multiple_of(x * SLAB, 16)
            fa[e, pl.ds(pl.multiple_of(base + SLAB, 8), SLAB), :] = basis_ref[e, pl.ds(base, SLAB), :].astype(F32)

    def sweep(src, dst, older):
        @pl.loop(0, BOX)
        def _(x):
            for e in range(EY):
                for t in range(SLAB // 8):
                    at = pl.multiple_of(x * SLAB + 8 * t, 8)
                    o = SLAB + at
                    center = src[e, pl.ds(o, 8), :]
                    beside = src[e, pl.ds(o - SLAB, 8), :] + src[e, pl.ds(o + SLAB, 8), :]
                    if t > 0:
                        v = src[e, pl.ds(o - BOX, 8), :]
                        beside = beside + (jnp.where(sub < 4, 0.0, v) if t == 1 else v)
                    if t < SLAB // 8 - 1:
                        v = src[e, pl.ds(o + BOX, 8), :]
                        beside = beside + (jnp.where(sub >= 4, 0.0, v) if t == SLAB // 8 - 2 else v)
                    v = src[e, pl.ds(o - 1, 8), :]
                    beside = beside + (v if t % 3 == 2 else jnp.where(sub == (0, 4)[t % 3], 0.0, v))
                    v = src[e, pl.ds(o + 1, 8), :]
                    beside = beside + (v if t % 3 == 0 else jnp.where(sub == (0, 3, 7)[t % 3], 0.0, v))
                    a = scaled[e, pl.ds(at, 8), :]
                    if older is None:
                        new = a * center - (0.5 / 5.5) * beside
                    else:
                        new = 2.0 * (a * center) - (1.0 / 5.5) * beside - older[e, pl.ds(o, 8), :]
                    dst[e, pl.ds(o, 8), :] = new

    sweep(fa, fb, None)
    sweep(fb, fa, fa)
    sweep(fa, fb, fb)

    for e in range(EY):
        full = fb[e, SLAB:SLAB + ROWS, :]
        high = full.astype(BF16)
        rest = (full - high.astype(F32)).astype(BF16)
        both = jnp.concatenate([high, rest], axis=1)
        prod = lax.dot_general(both, both, (((0,), (0,)), ((), ())), preferred_element_type=F32)
        cross = prod[0:NB, NB:2 * NB]
        gram[e] = prod[0:NB, 0:NB] + (cross + cross.T) + prod[NB:2 * NB, NB:2 * NB]

    factor_inverse([[gram[e, 8 * t:8 * t + 8, :] for t in range(BLOCKS)] for e in range(EY)], inv)

    up = jnp.where(sub == 0, 0.0, jnp.where((sub == 1) | (sub == 7), 0.25, 0.5))
    down = jnp.where(sub == 7, 0.0, jnp.where((sub == 0) | (sub == 6), 0.25, 0.5))

    def edge(i):
        return 0.25 if i in (0, 6) else 0.5

    for e in range(EY):
        for x in range(G):
            for y in range(G):
                p = (x + 2) * SLAB + (y + 2) * BOX + 2
                inner[e, 64 * x + 8 * y:64 * x + 8 * y + 8, :] = fb[e, SLAB + p:SLAB + p + 8, :]
    for e in range(EY):
        def tile(x, y):
            return inner[e, 64 * x + 8 * y:64 * x + 8 * y + 8, :]
        for x in range(G):
            for y in range(G):
                p = (x + 2) * SLAB + (y + 2) * BOX + 2
                c = tile(x, y)
                out = (5.5 * scaled[e, p:p + 8, :] + 6.5) * c
                if x > 0:
                    out = out - edge(x - 1) * tile(x - 1, y)
                if x < G - 1:
                    out = out - edge(x) * tile(x + 1, y)
                if y > 0:
                    out = out - edge(y - 1) * tile(x, y - 1)
                if y < G - 1:
                    out = out - edge(y) * tile(x, y + 1)
                out = out - up * pltpu.roll(c, 1, 0) - down * pltpu.roll(c, 7, 0)
                stencil[64 * x + 8 * y:64 * x + 8 * y + 8, :] = out
        raw = dot(inner[e], stencil[...], ((0,), (0,)))
        linv = inv[e]
        half = dot(linv, raw, ((1,), (0,)))
        diag = dot(half, linv, ((1,), (1,)))
        for r in range(BLOCKS):
            first_ref[r, e] = diag[8 * r:8 * r + 8, :]

        def layer(d, i):
            if d == 0:
                return inner[e, 64 * i:64 * i + 64, :]
            if d == 1:
                return jnp.concatenate([tile(x, i) for x in range(G)], axis=0)
            return inner[e, pl.ds(i, 64, stride=8), :]
        rows = []
        for d in range(3):
            last = layer(d, 7)
            rows += [-0.5 * last - 0.25 * layer(d, 6), -0.25 * last, layer(d, 0), layer(d, 1)]
        traces[e] = dot(jnp.concatenate(rows, axis=0), linv, ((1,), (1,)))
        for s, d in enumerate((0, 2)):
            left_ref[s, e] = traces[e, 256 * d:256 * d + 128, :]
            right_ref[s, e] = traces[e, 256 * d + 128:256 * d + 256, :]
    for e in range(EY):
        cy = dot(traces[e, 256:384, :], traces[1 - e, 384:512, :], ((0,), (0,)))
        for r in range(BLOCKS):
            first_ref[r, EY + e] = cy[8 * r:8 * r + 8, :]


def local_call(pot, basis):
    vm = pl.BlockSpec(memory_space=pltpu.VMEM)
    return pl.pallas_call(
        local_kernel,
        out_shape=(
            jax.ShapeDtypeStruct((BLOCKS, 2 * EY, 8, NB), F32),
            jax.ShapeDtypeStruct((2, EY, NB, NB), F32),
            jax.ShapeDtypeStruct((2, EY, NB, NB), F32),
        ),
        in_specs=[vm, vm],
        out_specs=(vm, vm, vm),
        scratch_shapes=[
            pltpu.VMEM((EY, ROWS, NB), F32),
            pltpu.VMEM((EY, ROWS + 2 * SLAB, NB), F32),
            pltpu.VMEM((EY, ROWS + 2 * SLAB, NB), F32),
            pltpu.VMEM((EY, G ** 3, NB), F32),
            pltpu.VMEM((G ** 3, NB), F32),
            pltpu.VMEM((EY, NB, NB), F32),
            pltpu.VMEM((EY, NB, NB), F32),
            pltpu.VMEM((EY, 768, NB), F32),
        ],
        compiler_params=pltpu.CompilerParams(vmem_limit_bytes=40 * 2**20),
    )(pot, basis)


def halo_kernel(block_ref, out_ref, low_x, high_x, low_z, high_z, corner, send_sem, recv_sem):
    ex, ez = lax.axis_index("ex"), lax.axis_index("ez")
    nx, nz = lax.axis_size("ex"), lax.axis_size("ez")
    xs = {-1: lax.rem(ex + nx - 1, nx), 0: ex, 1: lax.rem(ex + 1, nx)}
    zs = {-1: lax.rem(ez + nz - 1, nz), 0: ez, 1: lax.rem(ez + 1, nz)}
    steps = [(1, 0), (-1, 0), (0, 1), (0, -1), (1, 1), (1, -1), (-1, 1), (-1, -1)]
    barrier = pltpu.get_barrier_semaphore()
    for dx, dz in steps:
        pl.semaphore_signal(barrier, inc=1, device_id=(xs[dx], zs[dz]), device_id_type=MESH)
    pl.semaphore_wait(barrier, len(steps))
    landing = [low_x, high_x, low_z, high_z, corner.at[0], corner.at[1], corner.at[2], corner.at[3]]
    copies = []
    for n, (dx, dz) in enumerate(steps):
        if dx == 1:
            part = block_ref.at[pl.ds(G - 2, 2)]
        elif dx == -1:
            part = block_ref.at[pl.ds(0, 2)]
        else:
            part = block_ref
        copies.append(pltpu.make_async_remote_copy(
            src_ref=part, dst_ref=landing[n], send_sem=send_sem.at[n], recv_sem=recv_sem.at[n],
            device_id=(xs[dx], zs[dz]), device_id_type=MESH))
    for copy in copies:
        copy.start()
    for copy in copies:
        copy.wait()
    for x in range(BOX):
        if x < 2:
            low, mid, high = corner[0, x], low_x[x], corner[1, x]
        elif x < 2 + G:
            low, mid, high = low_z[x - 2], block_ref[x - 2], high_z[x - 2]
        else:
            low, mid, high = corner[2, x - 2 - G], high_x[x - 2 - G], corner[3, x - 2 - G]
        out_ref[x, 0:8, :] = jnp.concatenate([low[6:8], mid[0:6]], axis=0)
        out_ref[x, 8:16, :] = jnp.concatenate([mid[6:8], high[0:6]], axis=0)


def halo_call(block):
    vm = pl.BlockSpec(memory_space=pltpu.VMEM)
    part = (G, 2 * G)
    return pl.pallas_call(
        halo_kernel,
        out_shape=jax.ShapeDtypeStruct((BOX, 16, 2 * G), F32),
        in_specs=[vm],
        out_specs=vm,
        scratch_shapes=[
            pltpu.VMEM((2,) + part, F32),
            pltpu.VMEM((2,) + part, F32),
            pltpu.VMEM((G,) + part, F32),
            pltpu.VMEM((G,) + part, F32),
            pltpu.VMEM((4, 2) + part, F32),
            pltpu.SemaphoreType.DMA((8,)),
            pltpu.SemaphoreType.DMA((8,)),
        ],
        compiler_params=pltpu.CompilerParams(collective_id=0, has_side_effects=True),
    )(block)


def exchange_kernel(first_ref, left_ref, right_ref, diag_ref, coup_ref,
                    got_first, got_right, second, got_second,
                    right_send, right_recv, send_sem, recv_sem, own_sem):
    ex, ez = lax.axis_index("ex"), lax.axis_index("ez")
    nx, nz = lax.axis_size("ex"), lax.axis_size("ez")
    below, above = lax.rem(ex + nx - 1, nx), lax.rem(ex + 1, nx)
    peers = [lax.rem(ez + k, nz) for k in range(1, nz)]
    barrier = pltpu.get_barrier_semaphore()
    for target in [(below, ez), (above, ez)] + [(ex, p) for p in peers]:
        pl.semaphore_signal(barrier, inc=1, device_id=target, device_id_type=MESH)
    pl.semaphore_wait(barrier, nz + 1)

    traces = []
    for s, target in enumerate([(below, ez), (ex, peers[-1])]):
        traces.append(pltpu.make_async_remote_copy(
            src_ref=right_ref.at[s], dst_ref=got_right.at[s],
            send_sem=right_send.at[s], recv_sem=right_recv.at[s],
            device_id=target, device_id_type=MESH))
        traces[s].start()

    def spread(half, source, landing):
        copies = []
        for k, peer in enumerate(peers):
            copies.append(pltpu.make_async_remote_copy(
                src_ref=source.at[peer], dst_ref=landing.at[ez],
                send_sem=send_sem.at[half, k], recv_sem=recv_sem.at[half, k],
                device_id=(ex, peer), device_id_type=MESH))
            copies[k].start()
        own = pltpu.make_async_copy(source.at[ez], landing.at[ez], own_sem.at[half])
        own.start()
        return copies, own

    first_copies, first_own = spread(0, first_ref, got_first)
    for s in range(2):
        traces[s].wait_recv()
        for e in range(EY):
            block = dot(left_ref[s, e], got_right[s, e], ((0,), (0,)))
            for r in range(BLOCKS):
                second[r, s * EY + e] = block[8 * r:8 * r + 8, :]
    second_copies, second_own = spread(1, second, got_second)

    for copy in first_copies:
        copy.wait_recv()
    first_own.wait()

    @pl.loop(0, BLOCKS)
    def _(z):
        for e in range(EY):
            diag_ref[pl.ds(z * EY + e, 8, stride=BLOCKS * EY), :] = got_first[z, e]
            coup_ref[pl.ds(z * 3 * EY + EY + e, 8, stride=BLOCKS * 3 * EY), :] = got_first[z, EY + e]

    for copy in second_copies:
        copy.wait_recv()
    second_own.wait()

    @pl.loop(0, BLOCKS)
    def _(z):
        for e in range(EY):
            for s in range(2):
                coup_ref[pl.ds(z * 3 * EY + 2 * s * EY + e, 8, stride=BLOCKS * 3 * EY), :] = got_second[z, s * EY + e]

    for copy in traces + first_copies + second_copies:
        copy.wait_send()


def exchange_call(first, left, right):
    vm = pl.BlockSpec(memory_space=pltpu.VMEM)
    part = (BLOCKS, 2 * EY, 8, NB)
    return pl.pallas_call(
        exchange_kernel,
        out_shape=(
            jax.ShapeDtypeStruct((8 * BLOCKS * EY, NB), F32),
            jax.ShapeDtypeStruct((8 * BLOCKS * 3 * EY, NB), F32),
        ),
        in_specs=[vm] * 3,
        out_specs=(vm, vm),
        scratch_shapes=[
            pltpu.VMEM(part, F32),
            pltpu.VMEM((2, EY, NB, NB), F32),
            pltpu.VMEM(part, F32),
            pltpu.VMEM(part, F32),
            pltpu.SemaphoreType.DMA((2,)),
            pltpu.SemaphoreType.DMA((2,)),
            pltpu.SemaphoreType.DMA((2, BLOCKS - 1)),
            pltpu.SemaphoreType.DMA((2, BLOCKS - 1)),
            pltpu.SemaphoreType.DMA((2,)),
        ],
        compiler_params=pltpu.CompilerParams(collective_id=1, has_side_effects=True),
    )(first, left, right)


def local(potential, basis_start):
    halo = halo_call(jnp.transpose(potential, (0, 2, 1)))
    first, left, right = local_call(halo, basis_start.reshape(EY, ROWS, NB))
    diag, coup = exchange_call(first, left, right)
    coup = coup.reshape(8, BLOCKS, 3, EY, NB).transpose(0, 1, 3, 2, 4)
    return diag.reshape(1, 8, BLOCKS, EY, NB), coup[None]


def solution(mesh):
    return jax.shard_map(
        local,
        mesh=mesh,
        in_specs=(P("ex", None, "ez"), P("ex", "ez", None, None, None)),
        out_specs=(P("ex", "ez", None, None, None), P("ex", "ez", None, None, None, None)),
        check_vma=False,
    )
```

time: 152 us -> 69.8 us (0.46)
  Pallas kernels: 0 us -> 61.2 us
  other arithmetic: 56.1 us -> 0 us
  starting transfers between devices: 53.6 us -> 0 us
  waiting for transfers between devices: 15 us -> 0 us
  matrix products: 12.6 us -> 0 us
  loops' own time: 5.39 us -> 0 us
    pallas_call x0 -> x3, Pallas kernels: none -> 61.2 us  [the longest x1 28 us: halo_call(): pl.pallas_call(halo_kernel, out_shape=jax.ShapeDtypeStruct((BOX, 16, 2 *...]
    another operation x15 -> x0, other arithmetic: 45.8 us -> none  [the longest x6 24.8 us: local_basis(): factor = jnp.linalg.cholesky(intersection)]
    ppermute x6 -> x0, starting transfers between devices: 42.1 us -> none  [the longest x2 21.3 us: padded_2(): lax.ppermute(head, axis, [((i + 1) % count, i) for i in range(count)])]
    dot_general x9 -> x0, matrix products: 11.9 us -> none  [the longest x2 4.06 us: local_basis(): lax.dot_general(flattened, flattened, (((0,), (0,)), ((), ())), precision...]
    all_to_all x2 -> x0, starting transfers between devices: 11.5 us -> none  [the longest x1 7.53 us: local(): lax.all_to_all(diagonal, 'ez', split_axis=1, concat_axis=2, tiled=True)]
    all_to_all x2 -> x0, waiting for transfers between devices: 11.1 us -> none  [the longest x1 7.58 us: local(): lax.all_to_all(coupled, 'ez', split_axis=1, concat_axis=2, tiled=True)]
    another operation x1 -> x0, loops' own time: 5.39 us -> none  [local(): basis = lax.map(one_element, jnp.arange(y_elements, dtype=jnp.int32))]
    unnamed x3 -> x12, local copies, waits for them, and re-layouts: 2.64 us -> 7.57 us
  transfers between devices with their start and end apart: 8 -> 0, of which waited for: 4 -> 0; matrix products, arithmetic and copies ran while one was open for 7% -> 0% of each run, Pallas kernels for 0% -> 0%
where the time goes in v1:
time: 69.8 us; the launch traced here: 69.4 us
  Pallas kernels  61.2 us (88%)
  local copies, waits for them, and re-layouts  7.57 us (11%)
    pallas_call x1, Pallas kernels, halo_call(): pl.pallas_call(halo_kernel, out_shape=jax.ShapeDtypeStruct((BOX, 16, 2 *...  28 us
    pallas_call x1, Pallas kernels, exchange_call(): pl.pallas_call(exchange_kernel, out_shape=(jax.ShapeDtypeStruct((8 * BLOC...  19.9 us
    pallas_call x1, Pallas kernels, local_call(): pl.pallas_call(local_kernel, out_shape=(jax.ShapeDtypeStruct((BLOCKS, 2 *...  13.3 us
    unnamed x12, local copies, waits for them, and re-layouts  7.57 us

profile of v1, /device:TPU:1, one launch (start us, length us, event | category | flops | bytes accessed | tf_op | source)
XLA Modules:
  0.0 69.4 jit_solution(6399019371436582505)
XLA Ops:
  0.6 28.0 %shard_map.41.pot_ref = f32[12,16,16]{2,1,0:T(8,128)} custom-call(f32[8,8,16]{2,1,0:T(8,128)} %bitcast.11), custom_call_target="tpu_custom_call" | custom-call | tf_op jit(solution)/shard_map/pallas_call | solution.py:254
  28.6 0.0 copy-start
  28.6 1.2 %copy-done = bf16[1,1,2,1728,128]{4,3,2,1,0:T(8,128)(2,1)S(1)} copy-done((bf16[1,1,2,1728,128]{4,3,2,1,0:T(8,128)(2,1)S(1)}, bf16[1,1,2,1728,128]{4,3,2,1,0:T(8,128)(2,1)}, u32[]{:S(2)}) %copy-start) | copy-done | bytes 884760
  29.8 0.0 copy-start.1
  29.8 0.9 %copy-done.1 = f32[12,16,16]{2,1,0:T(8,128)S(1)} copy-done((f32[12,16,16]{2,1,0:T(8,128)S(1)}, f32[12,16,16]{2,1,0:T(8,128)}, u32[]{:S(2)}) %copy-start.1) | copy-done | bytes 12312
  30.7 13.3 %shard_map.42 = (f32[16,4,8,128]{3,2,1,0:T(8,128)S(1)}, f32[2,2,128,128]{3,2,1,0:T(8,128)S(1)}, f32[2,2,128,128]{3,2,1,0:T(8,128)S(1)}) custom-call(f32[12,16,16]{2,1,0:T(8,128)S(1)} %copy-done.1, bf16[2,1728,128]{2,1,0:T(8,128)(2,1)S(1)} %bitcast.8), custom_call_target="tpu_custom_call" | custom-call | tf_op jit(solution)/shard_map/pallas_call | solution.py:191
  44.0 0.0 copy-start.2
  44.0 0.7 copy-done.2
  44.7 0.0 copy-start.3
  44.7 0.7 %copy-done.3 = f32[2,2,128,128]{3,2,1,0:T(8,128)} copy-done((f32[2,2,128,128]{3,2,1,0:T(8,128)}, f32[2,2,128,128]{3,2,1,0:T(8,128)S(1)}, u32[]{:S(2)}) %copy-start.3) | copy-done | bytes 262168
  45.4 0.0 copy-start.4
  45.4 0.7 %copy-done.4 = f32[2,2,128,128]{3,2,1,0:T(8,128)} copy-done((f32[2,2,128,128]{3,2,1,0:T(8,128)}, f32[2,2,128,128]{3,2,1,0:T(8,128)S(1)}, u32[]{:S(2)}) %copy-start.4) | copy-done | bytes 262168
  46.1 19.9 %shard_map.43 = (f32[256,128]{1,0:T(8,128)}, f32[768,128]{1,0:T(8,128)}) custom-call(f32[16,4,8,128]{3,2,1,0:T(8,128)} %copy-done.2, f32[2,2,128,128]{3,2,1,0:T(8,128)} %copy-done.3, f32[2,2,128,128]{3,2,1,0:T(8,128)} %copy-done.4), custom_call_target="tpu_custom_call" | custom-call | tf_op jit(solution)/shard_map/pallas_call | solution.py:340
  66.0 1.6 %copy.6 = f32[1,8,16,2,128]{4,3,2,1,0:T(2,128)} copy(f32[1,8,16,2,128]{4,3,2,1,0:T(2,128)} %bitcast.10) | data formatting | bytes 262144
  67.6 1.8 %copy.7 = f32[1,8,16,2,3,128]{5,3,4,2,1,0:T(2,128)} copy(f32[1,8,16,2,3,128]{5,3,4,2,1,0:T(2,128)} %bitcast.9) | data formatting | bytes 786432
Async XLA Ops:
  28.6 1.2 %copy-start = (bf16[1,1,2,1728,128]{4,3,2,1,0:T(8,128)(2,1)S(1)}, bf16[1,1,2,1728,128]{4,3,2,1,0:T(8,128)(2,1)}, u32[]{:S(2)}) copy-start(bf16[1,1,2,1728,128]{4,3,2,1,0:T(8,128)(2,1)} %param.3) | copy-start | bytes 2654212
  29.8 0.9 %copy-start.1 = (f32[12,16,16]{2,1,0:T(8,128)S(1)}, f32[12,16,16]{2,1,0:T(8,128)}, u32[]{:S(2)}) copy-start(f32[12,16,16]{2,1,0:T(8,128)} %shard_map.41.pot_ref) | copy-start | bytes 36868
  44.0 0.7 %copy-start.2 = (f32[16,4,8,128]{3,2,1,0:T(8,128)}, f32[16,4,8,128]{3,2,1,0:T(8,128)S(1)}, u32[]{:S(2)}) copy-start(f32[16,4,8,128]{3,2,1,0:T(8,128)S(1)} %get-tuple-element.7.first_ref) | copy-start | bytes 786436
  44.7 0.7 %copy-start.3 = (f32[2,2,128,128]{3,2,1,0:T(8,128)}, f32[2,2,128,128]{3,2,1,0:T(8,128)S(1)}, u32[]{:S(2)}) copy-start(f32[2,2,128,128]{3,2,1,0:T(8,128)S(1)} %get-tuple-element.8.left_ref) | copy-start | bytes 786436
  45.4 0.7 %copy-start.4 = (f32[2,2,128,128]{3,2,1,0:T(8,128)}, f32[2,2,128,128]{3,2,1,0:T(8,128)S(1)}, u32[]{:S(2)}) copy-start(f32[2,2,128,128]{3,2,1,0:T(8,128)S(1)} %get-tuple-element.9.right_ref) | copy-start | bytes 786436

commit v2 on v1

v2 whole, which is shorter than its diff:
```python
import jax
import jax.numpy as jnp
from jax import lax
from jax.experimental import pallas as pl
from jax.experimental.pallas import tpu as pltpu
from jax.sharding import PartitionSpec as P

G, BOX, NB, EY = 8, 12, 128, 2
ROWS = BOX ** 3
SLAB = BOX * BOX
BLOCKS = NB // 8
HIGHEST = lax.Precision.HIGHEST
F32 = jnp.float32
BF16 = jnp.bfloat16
MESH = pl.DeviceIdType.MESH
SIDES = ((1, 0), (-1, 0), (0, 1), (0, -1), (1, 1), (1, -1), (-1, 1), (-1, -1))
PACKED = 9


def dot(a, b, dims):
    return lax.dot_general(a, b, (dims, ((), ())), precision=HIGHEST, preferred_element_type=F32)


def sub_row(tile, row):
    return jnp.broadcast_to(tile[row:row + 1, :], (8, NB))


def lane_col(tile, lane):
    return jnp.broadcast_to(tile[:, lane:lane + 1], (8, NB))


def factor_inverse(tiles_of, inv_ref):
    sub = lax.broadcasted_iota(jnp.int32, (8, NB), 0)
    lane = lax.broadcasted_iota(jnp.int32, (8, NB), 1)
    tiles = [list(t) for t in tiles_of]
    for k in range(BLOCKS):
        inside = (lane >= 8 * k) & (lane < 8 * k + 8)
        for e in range(len(tiles)):
            T = tiles[e]
            C = [lane_col(T[k], 8 * k + m) for m in range(8)]
            J = jnp.where(inside, jnp.where(lane - 8 * k == sub, 1.0, 0.0).astype(F32), T[k])
            forward = J
            rdiag = jnp.zeros((8, NB), F32)
            for j in range(8):
                r = 1.0 / sub_row(C[j], j)
                mult = jnp.where(sub == j, 0.0, C[j] * r)
                row = sub_row(J, j)
                forward = jnp.where(sub == j, J, forward)
                rdiag = jnp.where(sub == j, r, rdiag)
                for m in range(j + 1, 8):
                    C[m] = C[m] - mult * sub_row(C[m], j)
                J = J - mult * row
            J = J * rdiag
            inv_ref[e, 8 * k:8 * k + 8, :] = jnp.where(lane <= sub + 8 * k, forward * jnp.sqrt(rdiag), 0.0)
            if k + 1 < BLOCKS:
                rows = [sub_row(J, m) for m in range(8)]
                for t in range(k + 1, BLOCKS):
                    old = T[t]
                    new = jnp.where(inside, 0.0, old)
                    for m in range(8):
                        new = new - lane_col(old, 8 * k + m) * rows[m]
                    T[t] = new


def pack_lower(inv, packed, e):
    lane = lax.broadcasted_iota(jnp.int32, (8, NB), 1)
    for k in range(7):
        other = pltpu.roll(inv[e, 8 * (14 - k):8 * (15 - k), :], 8 * k + 8, 1)
        packed[e, k] = jnp.where(lane < 8 * k + 8, inv[e, 8 * k:8 * k + 8, :], other)
    packed[e, 7] = inv[e, 56:64, :]
    packed[e, 8] = inv[e, 120:128, :]


def unpack_lower(packed, s, e):
    lane = lax.broadcasted_iota(jnp.int32, (8, NB), 1)
    tiles = [None] * BLOCKS
    for k in range(7):
        tile = packed[s, e, k]
        tiles[k] = jnp.where(lane < 8 * k + 8, tile, 0.0)
        tiles[14 - k] = jnp.where(lane < 120 - 8 * k, pltpu.roll(tile, 120 - 8 * k, 1), 0.0)
    tiles[7] = packed[s, e, 7]
    tiles[15] = packed[s, e, 8]
    return jnp.concatenate(tiles, axis=0)


def main_kernel(pot_hbm, basis_ref, first_out, second_out,
                pot_ref, basis, low_x, high_x, low_z, high_z, corner,
                scaled, fa, fb, inner, stencil, gram, inv, face_z, got_face, packed, got_packed,
                crossed, first, second,
                basis_sem, halo_send, halo_recv, face_send, face_recv, pack_send, pack_recv,
                send_sem, recv_sem, own_sem):
    ex, ez = lax.axis_index("ex"), lax.axis_index("ez")
    nx, nz = lax.axis_size("ex"), lax.axis_size("ez")
    xs = {-1: lax.rem(ex + nx - 1, nx), 0: ex, 1: lax.rem(ex + 1, nx)}
    zs = {-1: lax.rem(ez + nz - 1, nz), 0: ez, 1: lax.rem(ez + 1, nz)}
    peers = [lax.rem(ez + k, nz) for k in range(1, nz)]
    loads = [pltpu.make_async_copy(basis_ref.at[e], basis.at[e], basis_sem.at[e]) for e in range(EY)]
    loads.append(pltpu.make_async_copy(pot_hbm, pot_ref, basis_sem.at[EY]))
    for load in loads:
        load.start()
    barrier = pltpu.get_barrier_semaphore()
    partners = [(ex, p) for p in peers] + [(xs[dx], zs[dz]) for dx, dz in SIDES if dx != 0]
    for target in partners:
        pl.semaphore_signal(barrier, inc=1, device_id=target, device_id_type=MESH)
    pl.semaphore_wait(barrier, len(partners))

    def send(source, landing, send_at, recv_at, target):
        copy = pltpu.make_async_remote_copy(
            src_ref=source, dst_ref=landing, send_sem=send_at, recv_sem=recv_at,
            device_id=target, device_id_type=MESH)
        copy.start()
        return copy

    landings = [low_x, high_x, low_z, high_z] + [corner.at[c] for c in range(4)]
    halo = []
    for n, (dx, dz) in enumerate(SIDES):
        part = pot_hbm if dx == 0 else pot_hbm.at[pl.ds(G - 2 if dx == 1 else 0, 2)]
        halo.append(send(part, landings[n], halo_send.at[n], halo_recv.at[n], (xs[dx], zs[dz])))

    sub = lax.broadcasted_iota(jnp.int32, (8, NB), 0)
    zero_slab = jnp.zeros((SLAB, NB), F32)
    for buf in (fa, fb):
        for e in range(EY):
            buf[e, 0:SLAB, :] = zero_slab
            buf[e, SLAB + ROWS:2 * SLAB + ROWS, :] = zero_slab
    for load in loads:
        load.wait()

    @pl.loop(0, BOX)
    def _(x):
        for e in range(EY):
            base = pl.multiple_of(x * SLAB, 16)
            fa[e, pl.ds(pl.multiple_of(base + SLAB, 8), SLAB), :] = basis[e, pl.ds(base, SLAB), :].astype(F32)

    for copy in halo:
        copy.wait_recv()

    def spread(x, low, mid, high):
        lower = (jnp.concatenate([low[6:8], mid[0:6]], axis=0) - 3.5) * (1.0 / 5.5)
        upper = (jnp.concatenate([mid[6:8], high[0:6]], axis=0) - 3.5) * (1.0 / 5.5)
        for y in range(16):
            a = jnp.broadcast_to(lower[:, y:y + 1], (8, NB))
            b = jnp.broadcast_to(upper[:, y:y + 1], (8, NB))
            for e in range(EY):
                at = (y - 8 * e + 2) % 16
                if at < BOX:
                    base = x * SLAB + at * BOX
                    scaled[e, pl.ds(base, 8), :] = a
                    scaled[e, pl.ds(base + 8, 4), :] = b[0:4, :]

    @pl.loop(0, 2)
    def _(x):
        spread(x, corner[0, x], low_x[x], corner[1, x])
        spread(x + 2 + G, corner[2, x], high_x[x], corner[3, x])

    @pl.loop(0, G)
    def _(x):
        spread(x + 2, low_z[x], pot_ref[x], high_z[x])

    def sweep(src, dst, older):
        @pl.loop(0, BOX)
        def _(x):
            for e in range(EY):
                for t in range(SLAB // 8):
                    at = pl.multiple_of(x * SLAB + 8 * t, 8)
                    o = SLAB + at
                    center = src[e, pl.ds(o, 8), :]
                    beside = src[e, pl.ds(o - SLAB, 8), :] + src[e, pl.ds(o + SLAB, 8), :]
                    if t > 0:
                        v = src[e, pl.ds(o - BOX, 8), :]
                        beside = beside + (jnp.where(sub < 4, 0.0, v) if t == 1 else v)
                    if t < SLAB // 8 - 1:
                        v = src[e, pl.ds(o + BOX, 8), :]
                        beside = beside + (jnp.where(sub >= 4, 0.0, v) if t == SLAB // 8 - 2 else v)
                    v = src[e, pl.ds(o - 1, 8), :]
                    beside = beside + (v if t % 3 == 2 else jnp.where(sub == (0, 4)[t % 3], 0.0, v))
                    v = src[e, pl.ds(o + 1, 8), :]
                    beside = beside + (v if t % 3 == 0 else jnp.where(sub == (0, 3, 7)[t % 3], 0.0, v))
                    a = scaled[e, pl.ds(at, 8), :]
                    if older is None:
                        new = a * center - (0.5 / 5.5) * beside
                    else:
                        new = 2.0 * (a * center) - (1.0 / 5.5) * beside - older[e, pl.ds(o, 8), :]
                    dst[e, pl.ds(o, 8), :] = new

    sweep(fa, fb, None)
    sweep(fb, fa, fa)
    sweep(fa, fb, fb)

    def corner_row(x, y):
        return (x + 2) * SLAB + (y + 2) * BOX + 2

    for e in range(EY):
        for x in range(G):
            for y in range(G):
                p = SLAB + corner_row(x, y)
                inner[e, 64 * x + 8 * y:64 * x + 8 * y + 8, :] = fb[e, p:p + 8, :]
        face_z[e, 0:64, :] = inner[e, pl.ds(0, 64, stride=8), :]
        face_z[e, 64:128, :] = inner[e, pl.ds(1, 64, stride=8), :]
    faces = []
    for e in range(EY):
        faces.append(send(inner.at[e, pl.ds(0, 128)], got_face.at[0, e], face_send.at[0, e], face_recv.at[0, e], (xs[-1], ez)))
        faces.append(send(face_z.at[e], got_face.at[1, e], face_send.at[1, e], face_recv.at[1, e], (ex, zs[-1])))

    for e in range(EY):
        full = fb[e, SLAB:SLAB + ROWS, :]
        high = full.astype(BF16)
        rest = (full - high.astype(F32)).astype(BF16)
        both = jnp.concatenate([high, rest], axis=1)
        prod = lax.dot_general(both, both, (((0,), (0,)), ((), ())), preferred_element_type=F32)
        cross = prod[0:NB, NB:2 * NB]
        gram[e] = prod[0:NB, 0:NB] + (cross + cross.T) + prod[NB:2 * NB, NB:2 * NB]

    up = jnp.where(sub == 0, 0.0, jnp.where((sub == 1) | (sub == 7), 0.25, 0.5))
    down = jnp.where(sub == 7, 0.0, jnp.where((sub == 0) | (sub == 6), 0.25, 0.5))

    def edge(i):
        return 0.25 if i in (0, 6) else 0.5

    def tile(e, x, y):
        return inner[e, 64 * x + 8 * y:64 * x + 8 * y + 8, :]

    def layer(e, d, i):
        if d == 0:
            return inner[e, 64 * i:64 * i + 64, :]
        if d == 1:
            return jnp.concatenate([tile(e, x, i) for x in range(G)], axis=0)
        return inner[e, pl.ds(i, 64, stride=8), :]

    def plus_side(e, d):
        last = layer(e, d, 7)
        return jnp.concatenate([-0.5 * last - 0.25 * layer(e, d, 6), -0.25 * last], axis=0)

    for e in range(EY):
        for x in range(G):
            for y in range(G):
                p = corner_row(x, y)
                c = tile(e, x, y)
                out = (5.5 * scaled[e, p:p + 8, :] + 6.5) * c
                if x > 0:
                    out = out - edge(x - 1) * tile(e, x - 1, y)
                if x < G - 1:
                    out = out - edge(x) * tile(e, x + 1, y)
                if y > 0:
                    out = out - edge(y - 1) * tile(e, x, y - 1)
                if y < G - 1:
                    out = out - edge(y) * tile(e, x, y + 1)
                out = out - up * pltpu.roll(c, 1, 0) - down * pltpu.roll(c, 7, 0)
                stencil[e, 64 * x + 8 * y:64 * x + 8 * y + 8, :] = out
        crossed[e, :, 0:NB] = dot(inner[e], stencil[e], ((0,), (0,)))
        minus_y = jnp.concatenate([layer(1 - e, 1, 0), layer(1 - e, 1, 1)], axis=0)
        crossed[e, :, NB:2 * NB] = dot(plus_side(e, 1), minus_y, ((0,), (0,)))

    factor_inverse([[gram[e, 8 * t:8 * t + 8, :] for t in range(BLOCKS)] for e in range(EY)], inv)

    packs = []
    for e in range(EY):
        pack_lower(inv, packed, e)
    for s, target in enumerate([(xs[-1], ez), (ex, zs[-1])]):
        packs.append(send(packed, got_packed.at[s], pack_send.at[s], pack_recv.at[s], target))

    def spread_rows(half, source, landing):
        copies = [send(source.at[p], landing.at[ez], send_sem.at[half, k], recv_sem.at[half, k], (ex, p))
                  for k, p in enumerate(peers)]
        own = pltpu.make_async_copy(source.at[ez], landing.at[ez], own_sem.at[half])
        own.start()
        return copies, own

    for e in range(EY):
        mixed = dot(inv[e], crossed[e, :, 0:2 * NB], ((1,), (0,)))
        diag = dot(mixed[:, 0:NB], inv[e], ((1,), (1,)))
        side = dot(mixed[:, NB:2 * NB], inv[1 - e], ((1,), (1,)))
        for r in range(BLOCKS):
            first[r, e] = diag[8 * r:8 * r + 8, :]
            first[r, EY + e] = side[8 * r:8 * r + 8, :]
    first_copies, first_own = spread_rows(0, first, first_out)

    for copy in faces:
        copy.wait_recv()
    for e in range(EY):
        raw = jnp.concatenate([dot(plus_side(e, 2 * s), got_face[s, e], ((0,), (0,))) for s in range(2)], axis=1)
        crossed[e, :, 0:2 * NB] = dot(inv[e], raw, ((1,), (0,)))
    for s in (1, 0):
        packs[s].wait_recv()
        for e in range(EY):
            block = dot(crossed[e, :, NB * s:NB * s + NB], unpack_lower(got_packed, s, e), ((1,), (1,)))
            for r in range(BLOCKS):
                second[r, s * EY + e] = block[8 * r:8 * r + 8, :]
    second_copies, second_own = spread_rows(1, second, second_out)

    for copy in first_copies + second_copies:
        copy.wait_recv()
    first_own.wait()
    second_own.wait()
    for copy in halo + faces + packs + first_copies + second_copies:
        copy.wait_send()


def main_call(block, starts):
    anywhere = pl.BlockSpec(memory_space=pl.ANY)
    hbm = pl.BlockSpec(memory_space=pltpu.HBM)
    part = (G, 2 * G)
    rows = (BLOCKS, 2 * EY, 8, NB)
    dma = pltpu.SemaphoreType.DMA
    return pl.pallas_call(
        main_kernel,
        out_shape=(jax.ShapeDtypeStruct(rows, F32), jax.ShapeDtypeStruct(rows, F32)),
        in_specs=[hbm, hbm],
        out_specs=(anywhere, anywhere),
        scratch_shapes=[
            pltpu.VMEM((G,) + part, F32),
            pltpu.VMEM((EY, ROWS, NB), BF16),
            pltpu.VMEM((2,) + part, F32),
            pltpu.VMEM((2,) + part, F32),
            pltpu.VMEM((G,) + part, F32),
            pltpu.VMEM((G,) + part, F32),
            pltpu.VMEM((4, 2) + part, F32),
            pltpu.VMEM((EY, ROWS, NB), F32),
            pltpu.VMEM((EY, ROWS + 2 * SLAB, NB), F32),
            pltpu.VMEM((EY, ROWS + 2 * SLAB, NB), F32),
            pltpu.VMEM((EY, G ** 3, NB), F32),
            pltpu.VMEM((EY, G ** 3, NB), F32),
            pltpu.VMEM((EY, NB, NB), F32),
            pltpu.VMEM((EY, NB, NB), F32),
            pltpu.VMEM((EY, NB, NB), F32),
            pltpu.VMEM((2, EY, NB, NB), F32),
            pltpu.VMEM((EY, PACKED, 8, NB), F32),
            pltpu.VMEM((2, EY, PACKED, 8, NB), F32),
            pltpu.VMEM((EY, NB, 2 * NB), F32),
            pltpu.VMEM(rows, F32),
            pltpu.VMEM(rows, F32),
            dma((EY + 1,)), dma((8,)), dma((8,)), dma((2, EY)), dma((2, EY)), dma((2,)), dma((2,)),
            dma((2, BLOCKS - 1)), dma((2, BLOCKS - 1)), dma((2,)),
        ],
        compiler_params=pltpu.CompilerParams(
            collective_id=0, has_side_effects=True, vmem_limit_bytes=40 * 2**20),
    )(block, starts)


def place_kernel(first_ref, second_ref, diag_ref, coup_ref):
    @pl.loop(0, BLOCKS)
    def _(z):
        for e in range(EY):
            diag_ref[pl.ds(z * EY + e, 8, stride=BLOCKS * EY), :] = first_ref[z, e]
            for k in range(3):
                tile = first_ref[z, EY + e] if k == 1 else second_ref[z, (k // 2) * EY + e]
                coup_ref[pl.ds(z * 3 * EY + k * EY + e, 8, stride=BLOCKS * 3 * EY), :] = tile


def place_call(first, second):
    vm = pl.BlockSpec(memory_space=pltpu.VMEM)
    return pl.pallas_call(
        place_kernel,
        out_shape=(
            jax.ShapeDtypeStruct((8 * BLOCKS * EY, NB), F32),
            jax.ShapeDtypeStruct((8 * BLOCKS * 3 * EY, NB), F32),
        ),
        in_specs=[vm, vm],
        out_specs=(vm, vm),
        compiler_params=pltpu.CompilerParams(vmem_limit_bytes=4 * 2**20),
    )(first, second)


def local(potential, basis_start):
    block = jnp.transpose(potential, (0, 2, 1))
    block = pltpu.with_memory_space_constraint(block, pltpu.HBM)
    starts = pltpu.with_memory_space_constraint(basis_start.reshape(EY, ROWS, NB), pltpu.HBM)
    first, second = main_call(block, starts)
    diag, coup = place_call(first, second)
    coup = coup.reshape(8, BLOCKS, 3, EY, NB).transpose(0, 1, 3, 2, 4)
    return diag.reshape(1, 8, BLOCKS, EY, NB), coup[None]


def solution(mesh):
    return jax.shard_map(
        local,
        mesh=mesh,
        in_specs=(P("ex", None, "ez"), P("ex", "ez", None, None, None)),
        out_specs=(P("ex", "ez", None, None, None), P("ex", "ez", None, None, None, None)),
        check_vma=False,
    )
```

time: 69.8 us -> 52 us (0.74)
  Pallas kernels: 61.2 us -> 51.2 us
  local copies, waits for them, and re-layouts: 7.57 us -> 0 us
    pallas_call x3 -> x2, Pallas kernels: 61.2 us -> 51.2 us  [the longest x1 50.1 us: main_call(): pl.pallas_call(main_kernel, out_shape=(jax.ShapeDtypeStruct(rows, F32), j...]
    unnamed x12 -> x0, local copies, waits for them, and re-layouts: 7.57 us -> none
where the time goes in v2:
time: 52 us; the launch traced here: 51.8 us
  Pallas kernels  51.2 us (98%)
  between operations  0.64 us (1%)
    pallas_call x1, Pallas kernels, main_call(): pl.pallas_call(main_kernel, out_shape=(jax.ShapeDtypeStruct(rows, F32), j...  50.1 us
    pallas_call x1, Pallas kernels, place_call(): pl.pallas_call(place_kernel, out_shape=(jax.ShapeDtypeStruct((8 * BLOCKS...  1.15 us

profile of v2, /device:TPU:1, one launch (start us, length us, event | category | flops | bytes accessed | tf_op | source)
XLA Modules:
  0.0 51.8 jit_solution(11871300290700806101)
XLA Ops:
  0.6 50.1 %shard_map.41 = (f32[16,4,8,128]{3,2,1,0:T(8,128)S(1)}, f32[16,4,8,128]{3,2,1,0:T(8,128)S(1)}) custom-call(f32[8,8,16]{2,1,0:T(8,128)} %bitcast.9, bf16[2,1728,128]{2,1,0:T(8,128)(2,1)} %bitcast.8), custom_call_target="tpu_custom_call" | custom-call | tf_op jit(solution)/shard_map/pallas_call | solution.py:305
  50.7 1.1 %shard_map.42 = (f32[256,128]{1,0:T(8,128)}, f32[768,128]{1,0:T(8,128)}) custom-call(f32[16,4,8,128]{3,2,1,0:T(8,128)S(1)} %get-tuple-element.6.first_ref, f32[16,4,8,128]{3,2,1,0:T(8,128)S(1)} %get-tuple-element.7.second_ref), custom_call_target="tpu_custom_call" | custom-call | tf_op jit(solution)/shard_map/pallas_call | solution.py:352

commit v3 on v2

--- a/solution.py
+++ b/solution.py
@@ -14,7 +14,7 @@
 BF16 = jnp.bfloat16
 MESH = pl.DeviceIdType.MESH
 SIDES = ((1, 0), (-1, 0), (0, 1), (0, -1), (1, 1), (1, -1), (-1, 1), (-1, -1))
-PACKED = 9
+PANEL = 4
 
 
 def dot(a, b, dims):
@@ -29,65 +29,73 @@
     return jnp.broadcast_to(tile[:, lane:lane + 1], (8, NB))
 
 
-def factor_inverse(tiles_of, inv_ref):
+def halves(a):
+    high = a.astype(BF16)
+    return high, (a - high.astype(F32)).astype(BF16)
+
+
+def dot3(a, b, dims):
+    (a_high, a_low), (b_high, b_low) = halves(a), halves(b)
+
+    def product(x, y):
+        return lax.dot_general(x, y, (dims, ((), ())), preferred_element_type=F32)
+    wide = product(jnp.concatenate([a_high, a_low], axis=dims[0][0]), jnp.concatenate([b_high, b_high], axis=dims[1][0]))
+    return wide + product(a_high, b_low)
+
+
+def factor_inverse(tiles_of, inv_ref, after_panel):
     sub = lax.broadcasted_iota(jnp.int32, (8, NB), 0)
     lane = lax.broadcasted_iota(jnp.int32, (8, NB), 1)
+    zero = jnp.zeros((8, NB), F32)
     tiles = [list(t) for t in tiles_of]
-    for k in range(BLOCKS):
-        inside = (lane >= 8 * k) & (lane < 8 * k + 8)
-        for e in range(len(tiles)):
-            T = tiles[e]
-            C = [lane_col(T[k], 8 * k + m) for m in range(8)]
-            J = jnp.where(inside, jnp.where(lane - 8 * k == sub, 1.0, 0.0).astype(F32), T[k])
-            forward = J
-            rdiag = jnp.zeros((8, NB), F32)
-            for j in range(8):
-                r = 1.0 / sub_row(C[j], j)
-                mult = jnp.where(sub == j, 0.0, C[j] * r)
-                row = sub_row(J, j)
-                forward = jnp.where(sub == j, J, forward)
-                rdiag = jnp.where(sub == j, r, rdiag)
-                for m in range(j + 1, 8):
-                    C[m] = C[m] - mult * sub_row(C[m], j)
-                J = J - mult * row
-            J = J * rdiag
-            inv_ref[e, 8 * k:8 * k + 8, :] = jnp.where(lane <= sub + 8 * k, forward * jnp.sqrt(rdiag), 0.0)
-            if k + 1 < BLOCKS:
+    for p in range(BLOCKS // PANEL):
+        first = PANEL * (p + 1)
+        full = [[None] * PANEL for _ in tiles]
+        for q in range(PANEL):
+            k = PANEL * p + q
+            inside = (lane >= 8 * k) & (lane < 8 * k + 8)
+            for e, T in enumerate(tiles):
+                C = [lane_col(T[k], 8 * k + m) for m in range(8)]
+                J = jnp.where(inside, jnp.where(lane - 8 * k == sub, 1.0, 0.0).astype(F32), T[k])
+                forward, rdiag = J, zero
+                for j in range(8):
+                    r = 1.0 / sub_row(C[j], j)
+                    mult = jnp.where(sub == j, 0.0, C[j] * r)
+                    row = sub_row(J, j)
+                    forward = jnp.where(sub == j, J, forward)
+                    rdiag = jnp.where(sub == j, r, rdiag)
+                    for m in range(j + 1, 8):
+                        C[m] = C[m] - mult * sub_row(C[m], j)
+                    J = J - mult * row
+                J = J * rdiag
+                inv_ref[e, 8 * k:8 * k + 8, :] = jnp.where(lane <= sub + 8 * k, forward * jnp.sqrt(rdiag), 0.0)
                 rows = [sub_row(J, m) for m in range(8)]
-                for t in range(k + 1, BLOCKS):
-                    old = T[t]
+
+                def update(old):
                     new = jnp.where(inside, 0.0, old)
                     for m in range(8):
                         new = new - lane_col(old, 8 * k + m) * rows[m]
-                    T[t] = new
-
-
-def pack_lower(inv, packed, e):
-    lane = lax.broadcasted_iota(jnp.int32, (8, NB), 1)
-    for k in range(7):
-        other = pltpu.roll(inv[e, 8 * (14 - k):8 * (15 - k), :], 8 * k + 8, 1)
-        packed[e, k] = jnp.where(lane < 8 * k + 8, inv[e, 8 * k:8 * k + 8, :], other)
-    packed[e, 7] = inv[e, 56:64, :]
-    packed[e, 8] = inv[e, 120:128, :]
-
-
-def unpack_lower(packed, s, e):
-    lane = lax.broadcasted_iota(jnp.int32, (8, NB), 1)
-    tiles = [None] * BLOCKS
-    for k in range(7):
-        tile = packed[s, e, k]
-        tiles[k] = jnp.where(lane < 8 * k + 8, tile, 0.0)
-        tiles[14 - k] = jnp.where(lane < 120 - 8 * k, pltpu.roll(tile, 120 - 8 * k, 1), 0.0)
-    tiles[7] = packed[s, e, 7]
-    tiles[15] = packed[s, e, 8]
-    return jnp.concatenate(tiles, axis=0)
-
-
-def main_kernel(pot_hbm, basis_ref, first_out, second_out,
+                    return new
+                for q2 in range(q + 1, PANEL):
+                    T[PANEL * p + q2] = update(T[PANEL * p + q2])
+                if first < BLOCKS:
+                    full[e][:q] = [update(old) for old in full[e][:q]]
+                    full[e][q] = J
+        after_panel(p)
+        if first < BLOCKS:
+            inside = (lane >= 8 * PANEL * p) & (lane < 8 * first)
+            for e, T in enumerate(tiles):
+                pivot = jnp.concatenate([zero] * (PANEL * p) + full[e] + [zero] * (BLOCKS - first), axis=0)
+                change = dot(jnp.concatenate(T[first:], axis=0), pivot, ((1,), (0,)))
+                for t in range(first, BLOCKS):
+                    T[t] = jnp.where(inside, 0.0, T[t]) - change[8 * (t - first):8 * (t - first) + 8, :]
+
+
+def main_kernel(pot_hbm, basis_ref, first_out, second_out, third_out,
                 pot_ref, basis, low_x, high_x, low_z, high_z, corner,
-                scaled, fa, fb, inner, stencil, gram, inv, face_z, got_face, packed, got_packed,
-                crossed, first, second,
-                basis_sem, halo_send, halo_recv, face_send, face_recv, pack_send, pack_recv,
+                scaled, fa, fb, inner, stencil, gram, inv, minus, plus, turned, got_turned,
+                crossed, first, second, third,
+                basis_sem, halo_send, halo_recv, turn_send, turn_recv,
                 send_sem, recv_sem, own_sem):
     ex, ez = lax.axis_index("ex"), lax.axis_index("ez")
     nx, nz = lax.axis_size("ex"), lax.axis_size("ez")
@@ -195,12 +203,6 @@
             for y in range(G):
                 p = SLAB + corner_row(x, y)
                 inner[e, 64 * x + 8 * y:64 * x + 8 * y + 8, :] = fb[e, p:p + 8, :]
-        face_z[e, 0:64, :] = inner[e, pl.ds(0, 64, stride=8), :]
-        face_z[e, 64:128, :] = inner[e, pl.ds(1, 64, stride=8), :]
-    faces = []
-    for e in range(EY):
-        faces.append(send(inner.at[e, pl.ds(0, 128)], got_face.at[0, e], face_send.at[0, e], face_recv.at[0, e], (xs[-1], ez)))
-        faces.append(send(face_z.at[e], got_face.at[1, e], face_send.at[1, e], face_recv.at[1, e], (ex, zs[-1])))
 
     for e in range(EY):
         full = fb[e, SLAB:SLAB + ROWS, :]
@@ -251,48 +253,58 @@
         minus_y = jnp.concatenate([layer(1 - e, 1, 0), layer(1 - e, 1, 1)], axis=0)
         crossed[e, :, NB:2 * NB] = dot(plus_side(e, 1), minus_y, ((0,), (0,)))
 
-    factor_inverse([[gram[e, 8 * t:8 * t + 8, :] for t in range(BLOCKS)] for e in range(EY)], inv)
-
-    packs = []
-    for e in range(EY):
-        pack_lower(inv, packed, e)
-    for s, target in enumerate([(xs[-1], ez), (ex, zs[-1])]):
-        packs.append(send(packed, got_packed.at[s], pack_send.at[s], pack_recv.at[s], target))
-
-    def spread_rows(half, source, landing):
-        copies = [send(source.at[p], landing.at[ez], send_sem.at[half, k], recv_sem.at[half, k], (ex, p))
+    for e in range(EY):
+        for s in range(2):
+            minus[e, 128 * s:128 * s + 64, :] = layer(e, 2 * s, 0)
+            minus[e, 128 * s + 64:128 * s + 128, :] = layer(e, 2 * s, 1)
+            plus[e, 128 * s:128 * s + 128, :] = plus_side(e, 2 * s)
+    turns = []
+
+    def send_turned(p):
+        rows = 8 * PANEL
+        for e in range(EY):
+            part = dot3(inv[e, rows * p:rows * p + rows, :], minus[e], ((1,), (1,)))
+            for s in range(2):
+                turned[s, p, e] = part[:, NB * s:NB * s + NB]
+        for s, target in enumerate([(xs[-1], ez), (ex, zs[-1])]):
+            turns.append(send(turned.at[s, p], got_turned.at[s, p], turn_send.at[s, p], turn_recv.at[s, p], target))
+
+    factor_inverse([[gram[e, 8 * t:8 * t + 8, :] for t in range(BLOCKS)] for e in range(EY)], inv, send_turned)
+
+    def spread_rows(part, source, landing):
+        copies = [send(source.at[p], landing.at[ez], send_sem.at[part, k], recv_sem.at[part, k], (ex, p))
                   for k, p in enumerate(peers)]
-        own = pltpu.make_async_copy(source.at[ez], landing.at[ez], own_sem.at[half])
+        own = pltpu.make_async_copy(source.at[ez], landing.at[ez], own_sem.at[part])
         own.start()
         return copies, own
 
     for e in range(EY):
-        mixed = dot(inv[e], crossed[e, :, 0:2 * NB], ((1,), (0,)))
-        diag = dot(mixed[:, 0:NB], inv[e], ((1,), (1,)))
-        side = dot(mixed[:, NB:2 * NB], inv[1 - e], ((1,), (1,)))
+        mixed = dot3(inv[e], crossed[e, :, 0:2 * NB], ((1,), (0,)))
+        diag = dot3(mixed[:, 0:NB], inv[e], ((1,), (1,)))
+        side = dot3(mixed[:, NB:2 * NB], inv[1 - e], ((1,), (1,)))
         for r in range(BLOCKS):
             first[r, e] = diag[8 * r:8 * r + 8, :]
             first[r, EY + e] = side[8 * r:8 * r + 8, :]
     first_copies, first_own = spread_rows(0, first, first_out)
 
-    for copy in faces:
-        copy.wait_recv()
-    for e in range(EY):
-        raw = jnp.concatenate([dot(plus_side(e, 2 * s), got_face[s, e], ((0,), (0,))) for s in range(2)], axis=1)
-        crossed[e, :, 0:2 * NB] = dot(inv[e], raw, ((1,), (0,)))
-    for s in (1, 0):
-        packs[s].wait_recv()
-        for e in range(EY):
-            block = dot(crossed[e, :, NB * s:NB * s + NB], unpack_lower(got_packed, s, e), ((1,), (1,)))
+    for e in range(EY):
+        crossed[e] = dot3(inv[e], plus[e], ((1,), (1,)))
+    parts = [(first_copies, first_own)]
+    for s, source, landing in ((1, third, third_out), (0, second, second_out)):
+        for copy in turns[s::2]:
+            copy.wait_recv()
+        for e in range(EY):
+            other = jnp.concatenate([got_turned[s, p, e] for p in range(BLOCKS // PANEL)], axis=0)
+            block = dot3(crossed[e, :, NB * s:NB * s + NB], other, ((1,), (1,)))
             for r in range(BLOCKS):
-                second[r, s * EY + e] = block[8 * r:8 * r + 8, :]
-    second_copies, second_own = spread_rows(1, second, second_out)
-
-    for copy in first_copies + second_copies:
-        copy.wait_recv()
-    first_own.wait()
-    second_own.wait()
-    for copy in halo + faces + packs + first_copies + second_copies:
+                source[r, e] = block[8 * r:8 * r + 8, :]
+        parts.append(spread_rows(1 + s, source, landing))
+
+    for copies, own in parts:
+        for copy in copies:
+            copy.wait_recv()
+        own.wait()
+    for copy in halo + turns + [copy for copies, _ in parts for copy in copies]:
         copy.wait_send()
 
 
@@ -300,13 +312,14 @@
     anywhere = pl.BlockSpec(memory_space=pl.ANY)
     hbm = pl.BlockSpec(memory_space=pltpu.HBM)
     part = (G, 2 * G)
-    rows = (BLOCKS, 2 * EY, 8, NB)
+    panels = (2, BLOCKS // PANEL, EY, 8 * PANEL, NB)
+    rows, half = (BLOCKS, 2 * EY, 8, NB), (BLOCKS, EY, 8, NB)
     dma = pltpu.SemaphoreType.DMA
     return pl.pallas_call(
         main_kernel,
-        out_shape=(jax.ShapeDtypeStruct(rows, F32), jax.ShapeDtypeStruct(rows, F32)),
+        out_shape=tuple(jax.ShapeDtypeStruct(r, F32) for r in (rows, half, half)),
         in_specs=[hbm, hbm],
-        out_specs=(anywhere, anywhere),
+        out_specs=(anywhere,) * 3,
         scratch_shapes=[
             pltpu.VMEM((G,) + part, F32),
             pltpu.VMEM((EY, ROWS, NB), BF16),
@@ -322,32 +335,33 @@
             pltpu.VMEM((EY, G ** 3, NB), F32),
             pltpu.VMEM((EY, NB, NB), F32),
             pltpu.VMEM((EY, NB, NB), F32),
-            pltpu.VMEM((EY, NB, NB), F32),
-            pltpu.VMEM((2, EY, NB, NB), F32),
-            pltpu.VMEM((EY, PACKED, 8, NB), F32),
-            pltpu.VMEM((2, EY, PACKED, 8, NB), F32),
+            pltpu.VMEM((EY, 2 * NB, NB), F32),
+            pltpu.VMEM((EY, 2 * NB, NB), F32),
+            pltpu.VMEM(panels, F32),
+            pltpu.VMEM(panels, F32),
             pltpu.VMEM((EY, NB, 2 * NB), F32),
             pltpu.VMEM(rows, F32),
-            pltpu.VMEM(rows, F32),
-            dma((EY + 1,)), dma((8,)), dma((8,)), dma((2, EY)), dma((2, EY)), dma((2,)), dma((2,)),
-            dma((2, BLOCKS - 1)), dma((2, BLOCKS - 1)), dma((2,)),
+            pltpu.VMEM(half, F32),
+            pltpu.VMEM(half, F32),
+            dma((EY + 1,)), dma((8,)), dma((8,)), dma((2, BLOCKS // PANEL)), dma((2, BLOCKS // PANEL)),
+            dma((3, BLOCKS - 1)), dma((3, BLOCKS - 1)), dma((3,)),
         ],
         compiler_params=pltpu.CompilerParams(
             collective_id=0, has_side_effects=True, vmem_limit_bytes=40 * 2**20),
     )(block, starts)
 
 
-def place_kernel(first_ref, second_ref, diag_ref, coup_ref):
+def place_kernel(first_ref, second_ref, third_ref, diag_ref, coup_ref):
     @pl.loop(0, BLOCKS)
     def _(z):
         for e in range(EY):
             diag_ref[pl.ds(z * EY + e, 8, stride=BLOCKS * EY), :] = first_ref[z, e]
             for k in range(3):
-                tile = first_ref[z, EY + e] if k == 1 else second_ref[z, (k // 2) * EY + e]
+                tile = (second_ref[z, e], first_ref[z, EY + e], third_ref[z, e])[k]
                 coup_ref[pl.ds(z * 3 * EY + k * EY + e, 8, stride=BLOCKS * 3 * EY), :] = tile
 
 
-def place_call(first, second):
+def place_call(*parts):
     vm = pl.BlockSpec(memory_space=pltpu.VMEM)
     return pl.pallas_call(
         place_kernel,
@@ -355,18 +369,17 @@
             jax.ShapeDtypeStruct((8 * BLOCKS * EY, NB), F32),
             jax.ShapeDtypeStruct((8 * BLOCKS * 3 * EY, NB), F32),
         ),
-        in_specs=[vm, vm],
+        in_specs=[vm] * 3,
         out_specs=(vm, vm),
         compiler_params=pltpu.CompilerParams(vmem_limit_bytes=4 * 2**20),
-    )(first, second)
+    )(*parts)
 
 
 def local(potential, basis_start):
     block = jnp.transpose(potential, (0, 2, 1))
     block = pltpu.with_memory_space_constraint(block, pltpu.HBM)
     starts = pltpu.with_memory_space_constraint(basis_start.reshape(EY, ROWS, NB), pltpu.HBM)
-    first, second = main_call(block, starts)
-    diag, coup = place_call(first, second)
+    diag, coup = place_call(*main_call(block, starts))
     coup = coup.reshape(8, BLOCKS, 3, EY, NB).transpose(0, 1, 3, 2, 4)
     return diag.reshape(1, 8, BLOCKS, EY, NB), coup[None]
 

time: 52 us -> 49.9 us (0.960)
  Pallas kernels: 51.2 us -> 49.1 us
    pallas_call x1, Pallas kernels: 50.1 us -> 48 us  [main_call(): pl.pallas_call(main_kernel, out_shape=tuple((jax.ShapeDtypeStruct(r, F32)...]
where the time goes in v3:
time: 49.9 us; the launch traced here: 49.8 us
  Pallas kernels  49.1 us (98%)
  between operations  0.64 us (1%)
    pallas_call x1, Pallas kernels, main_call(): pl.pallas_call(main_kernel, out_shape=tuple((jax.ShapeDtypeStruct(r, F32)...  48 us
    pallas_call x1, Pallas kernels, place_call(): pl.pallas_call(place_kernel, out_shape=(jax.ShapeDtypeStruct((8 * BLOCKS...  1.15 us

profile of v3, /device:TPU:1, one launch (start us, length us, event | category | flops | bytes accessed | tf_op | source)
XLA Modules:
  0.0 49.8 jit_solution(726803602048822746)
XLA Ops:
  0.6 48.0 %shard_map.41 = (f32[16,4,8,128]{3,2,1,0:T(8,128)S(1)}, f32[16,2,8,128]{3,2,1,0:T(8,128)S(1)}, f32[16,2,8,128]{3,2,1,0:T(8,128)S(1)}) custom-call(f32[8,8,16]{2,1,0:T(8,128)} %bitcast.9, bf16[2,1728,128]{2,1,0:T(8,128)(2,1)} %bitcast.8), custom_call_target="tpu_custom_call" | custom-call | tf_op jit(solution)/shard_map/pallas_call | solution.py:318
  48.6 1.1 %shard_map.42 = (f32[256,128]{1,0:T(8,128)}, f32[768,128]{1,0:T(8,128)}) custom-call(f32[16,4,8,128]{3,2,1,0:T(8,128)S(1)} %get-tuple-element.7.first_ref, f32[16,2,8,128]{3,2,1,0:T(8,128)S(1)} %get-tuple-element.8.second_ref, f32[16,2,8,128]{3,2,1,0:T(8,128)S(1)} %get-tuple-element.9.third_ref), custom_call_target="tpu_custom_call" | custom-call | tf_op jit(solution)/shard_map/pallas_call | solution.py:366
